TPU v7x, 32 devices: a whole 2x2x4 slice. The times are simulated.
32 devices in a mesh: cuts: 2 (over x), outer: 16 (over z, y, core).
Axes of the slice: x: 2, y: 2, z: 4, core: 2. Of those that a mesh axis runs over, the one named last changes fastest.
Arguments:
- stem_tensor: bfloat16 [32, 512, 2, 512], P(('cuts', 'outer')), parts along dimension 0, may hold values from -6 to 6
- leaf_left: bfloat16 [4, 2, 8192, 2, 512], P(None, None, 'outer'), may hold values from -0.09375 to 0.09375
- leaf_right: bfloat16 [4, 2, 8192, 2, 512], P(None, None, 'outer'), may hold values from -0.125 to 0.125
- slice_bits: int32 [8], P('cuts'), parts along dimension 0, may hold values from 0 to 1, as said below
Outputs:
- stem_out: bfloat16 [32, 512, 2, 512], P(('cuts', 'outer')), parts along dimension 0
There are 2 independent parts, one for each index of `cuts`. A program takes and returns all parts, laid end to end along the dimension named above; an argument that names none is the same for every part. Nothing has to cross between parts.
Inputs may be any that keep to these rules, and one draw needn't show every extreme that they name: `slice_bits`: the first entry is the index of the part modulo 2, so neighbouring parts contract different slices; the other entries are drawn independently.
All inputs are finite; a program needn't handle non-finite values.
Results may differ from a plain program's by a relative error of at most 0.01.
Values may be sent and summed in bfloat16 or wider, within the bound.
A program may use at most 64 MiB of HBM per device.

v0:
```python
import jax
import jax.numpy as jnp
from jax import lax
from jax.sharding import PartitionSpec as P

ROUNDS = 2


def leaf_term(left_leaf, right_leaf, row_count):
    depth = left_leaf.shape[0]
    width = right_leaf.shape[2]
    product = lax.dot_general(
        left_leaf.reshape(depth, 2 * row_count),
        right_leaf.reshape(depth, 2 * width),
        (((0,), (0,)), ((), ())),
        preferred_element_type=jnp.float32,
    )
    product = product.reshape(2, row_count, 2, width)
    real_part = product[0, :, 0] - product[1, :, 1]
    imag_part = product[0, :, 1] + product[1, :, 0]
    return jnp.stack([real_part, imag_part], axis=1)


def absorb_columns(stem_tile, q_branch):
    width = q_branch.shape[0]
    q_flat = q_branch.reshape(width, 2 * width)
    from_real = jnp.dot(stem_tile[:, 0, :], q_flat, preferred_element_type=jnp.float32)
    from_imag = jnp.dot(stem_tile[:, 1, :], q_flat, preferred_element_type=jnp.float32)
    real_part = from_real[:, :width] - from_imag[:, width:]
    imag_part = from_real[:, width:] + from_imag[:, :width]
    return jnp.stack([real_part, imag_part], axis=1).astype(jnp.bfloat16)


def on_device(stem_tensor, leaf_left, leaf_right, slice_bits):
    width = stem_tensor.shape[1]
    state = stem_tensor
    for round_index in range(ROUNDS):
        leaves = []
        for branch_index in (2 * round_index, 2 * round_index + 1):
            chosen = slice_bits[branch_index]
            leaves.append(
                (
                    lax.dynamic_index_in_dim(leaf_left[branch_index], chosen, 0, keepdims=False),
                    lax.dynamic_index_in_dim(leaf_right[branch_index], chosen, 0, keepdims=False),
                )
            )
        totals = lax.psum(
            (
                leaf_term(leaves[0][0], leaves[0][1], width),
                leaf_term(leaves[1][0], leaves[1][1], width),
            ),
            "outer",
        )
        p_branch = totals[0].astype(jnp.bfloat16)
        q_branch = totals[1].astype(jnp.bfloat16)
        absorbed = absorb_columns(state[0], q_branch)[None]
        p_flat = p_branch.reshape(width, 2 * width)
        received = lax.all_to_all(absorbed, "outer", split_axis=1, concat_axis=0, tiled=True)
        items = received.shape[3]
        regrouped = received.reshape(width, 2, items)
        from_real = lax.dot_general(
            p_flat, regrouped[:, 0, :], (((0,), (0,)), ((), ())), preferred_element_type=jnp.float32
        )
        from_imag = lax.dot_general(
            p_flat, regrouped[:, 1, :], (((0,), (0,)), ((), ())), preferred_element_type=jnp.float32
        )
        real_part = from_real[:width] - from_imag[width:]
        imag_part = from_real[width:] + from_imag[:width]
        renewed = jnp.stack([real_part, imag_part], axis=1).astype(jnp.bfloat16)
        state = renewed[None]
    return state


def solution(mesh):
    return jax.shard_map(
        on_device,
        mesh=mesh,
        in_specs=(
            P(("cuts", "outer"), None, None, None),
            P(None, None, "outer", None, None),
            P(None, None, "outer", None, None),
            P("cuts"),
        ),
        out_specs=P(("cuts", "outer"), None, None, None),
        check_vma=False,
    )
```

profile of v0, /device:TPU:1, one launch (start us, length us, event | category | flops | bytes accessed | tf_op | source)
XLA Modules:
  0.0 340.8 jit_solution(12925352407086176754)
XLA Ops:
  0.0 1.4 fusion.44
  6.3 8.9 %fusion.42 = (bf16[1,2,512,2,512]{4,3,2,1,0:T(2,128)(2,1)S(1)}, bf16[1,2,512,2,512]{4,3,2,1,0:T(2,128)(2,1)}, bf16[1,2,512,2,512]{4,3,2,1,0:T(2,128)(2,1)}, bf16[1,2,512,2,512]{4,3,2,1,0:T(2,128)(2,1)}) fusion(bf16[4,2,512,2,512]{4,3,2,1,0:T(2,128)(2,1)} %param.5), kind=kLoop, calls=%fused_computation.82 | loop fusion | bytes 16777216 | tf_op jit(solution)/shard_map/slice | solution.py:43
  16.6 3.6 %constant_dynamic-slice_fusion.1 = (bf16[1,1,512,2,512]{4,3,2,1,0:T(2,128)(2,1)S(1)}, bf16[1,1,512,2,512]{4,3,2,1,0:T(2,128)(2,1)}) fusion(bf16[1,2,512,2,512]{4,3,2,1,0:T(2,128)(2,1)} %get-tuple-element.12, s32[]{:T(128)S(6)} %select_n.20, bf16[1,2,512,2,512]{4,3,2,1,0:T(2,128)(2,1)S(1)} %get-tuple-element.9, s32[]{:T(128)S(6)} %select_n.19), kind=kLoop, calls=%fused_computation.75 | loop fusion | bytes 4194312 | tf_op jit(solution)/shard_map/jit(dynamic_index_in_dim)/dynamic_slice | solution.py:43
  20.2 2.4 copy.67
  22.6 8.8 %fusion.43 = (bf16[1,2,512,2,512]{4,3,2,1,0:T(2,128)(2,1)S(1)}, bf16[1,2,512,2,512]{4,3,2,1,0:T(2,128)(2,1)}, bf16[1,2,512,2,512]{4,3,2,1,0:T(2,128)(2,1)}, bf16[1,2,512,2,512]{4,3,2,1,0:T(2,128)(2,1)S(1)}) fusion(bf16[4,2,512,2,512]{4,3,2,1,0:T(2,128)(2,1)} %param.6), kind=kLoop, calls=%fused_computation.83 | loop fusion | bytes 16777216 | tf_op jit(solution)/shard_map/slice | solution.py:44
  31.5 2.4 constant_dynamic-slice_fusion
  33.9 2.5 copy.69
  36.4 2.5 fusion.19
  38.9 0.5 fusion.11
  40.8 4.4 %constant_dynamic-slice_fusion.5 = (bf16[1,1,512,2,512]{4,3,2,1,0:T(2,128)(2,1)}, bf16[1,1,512,2,512]{4,3,2,1,0:T(2,128)(2,1)}) fusion(bf16[1,2,512,2,512]{4,3,2,1,0:T(2,128)(2,1)} %get-tuple-element.10, s32[]{:T(128)S(6)} %select_n.18, bf16[1,2,512,2,512]{4,3,2,1,0:T(2,128)(2,1)} %get-tuple-element.11, s32[]{:T(128)S(6)} %select_n.17), kind=kLoop, calls=%fused_computation.79 | loop fusion | bytes 4194312 | tf_op jit(solution)/shard_map/jit(dynamic_index_in_dim)/dynamic_slice | solution.py:43
  45.1 3.7 %copy.63 = bf16[1,1,512,2,512]{2,4,3,1,0:T(8,128)(2,1)} copy(bf16[1,1,512,2,512]{4,3,2,1,0:T(2,128)(2,1)} %get-tuple-element.41) | data formatting | bytes 2097152
  48.8 4.3 %constant_dynamic-slice_fusion.4 = (bf16[1,1,512,2,512]{4,3,2,1,0:T(2,128)(2,1)}, bf16[1,1,512,2,512]{4,3,2,1,0:T(2,128)(2,1)}) fusion(bf16[1,2,512,2,512]{4,3,2,1,0:T(2,128)(2,1)} %get-tuple-element.14, s32[]{:T(128)S(6)} %select_n.18, bf16[1,2,512,2,512]{4,3,2,1,0:T(2,128)(2,1)} %get-tuple-element.15, s32[]{:T(128)S(6)} %select_n.17), kind=kLoop, calls=%fused_computation.78 | loop fusion | bytes 4194312 | tf_op jit(solution)/shard_map/jit(dynamic_index_in_dim)/dynamic_slice | solution.py:44
  53.1 3.7 %copy.65 = bf16[1,1,512,2,512]{2,4,3,1,0:T(8,128)(2,1)} copy(bf16[1,1,512,2,512]{4,3,2,1,0:T(2,128)(2,1)} %get-tuple-element.37) | data formatting | bytes 2097152
  56.8 2.8 fusion.22
  59.6 0.5 fusion.13
  60.1 1.5 pad_maximum_fusion.1
  61.6 2.5 copy.71
  64.1 3.7 %copy.73 = bf16[1,1,512,2,512]{2,4,3,1,0:T(8,128)(2,1)} copy(bf16[1,1,512,2,512]{4,3,2,1,0:T(2,128)(2,1)} %get-tuple-element.35) | data formatting | bytes 2097152
  67.8 2.5 fusion.16
  70.8 1.5 pad_maximum_fusion.3
  72.3 2.5 copy.59
  74.8 3.7 %copy.61 = bf16[1,1,512,2,512]{2,4,3,1,0:T(8,128)(2,1)} copy(bf16[1,1,512,2,512]{4,3,2,1,0:T(2,128)(2,1)} %get-tuple-element.38) | data formatting | bytes 2097152
  78.6 2.5 fusion.25
  81.6 1.5 pad_maximum_fusion
  83.1 185.5 %all-reduce.2 = (bf16[512,2,512]{2,0,1:T(8,128)(2,1)}, bf16[512,2,512]{2,0,1:T(8,128)(2,1)}, bf16[512,2,512]{2,0,1:T(8,128)(2,1)}, bf16[512,2,512]{2,0,1:T(8,128)(2,1)S(1)}) all-reduce(f32[512,2,512]{2,0,1:T(8,128)} %pad_maximum_fusion, f32[512,2,512]{2,0,1:T(8,128)} %pad_maximum_fusion.3, ...), channel_id=1, replica_groups=mesh['cuts'=2,'outer'=16] {'outer'}, use_global_device_ids=true, to_apply=%region_0.1 | all-reduce | flops 2097152 | bytes 12582912 | tf_op jit(solution)/shard_map/psum | solution.py:47
  268.5 0.5 copy.44
  269.1 0.7 copy-done.3
  269.9 0.7 convolution_bitcast_fusion
  270.7 0.7 convolution_bitcast_fusion.1
  271.4 0.6 fusion.28
  272.1 2.1 copy.46
  274.2 3.9 %all-to-all-start = ((bf16[1,512,2,512]{3,2,0,1:T(2,128)(2,1)}), bf16[1,512,2,512]{3,2,0,1:T(2,128)(2,1)S(1)}, u32[]{:S(2)}, u32[]{:S(2)}) async-start(bf16[1,512,2,512]{3,2,0,1:T(2,128)(2,1)} %copy.46), calls=%async_computation | async-start | bytes 2097152 | tf_op jit(solution)/shard_map/all_to_all | solution.py:58
  278.1 0.5 copy.41
  278.7 1.5 copy.50
  280.2 20.6 %all-to-all-done = bf16[1,512,2,512]{3,2,0,1:T(2,128)(2,1)S(1)} async-done(((bf16[1,512,2,512]{3,2,0,1:T(2,128)(2,1)}), bf16[1,512,2,512]{3,2,0,1:T(2,128)(2,1)S(1)}, u32[]{:S(2)}, u32[]{:S(2)}) %all-to-all-start) | async-done | bytes 1048608 | tf_op jit(solution)/shard_map/all_to_all | solution.py:58
  301.0 0.7 fusion.41
  301.7 0.7 fusion.40
  302.4 0.8 fusion.30
  303.2 0.8 fusion.32
  304.0 0.6 fusion.34
  304.7 2.1 copy.51
  306.7 6.5 %all-to-all-start.1 = ((bf16[1,512,2,512]{3,2,0,1:T(2,128)(2,1)}), bf16[1,512,2,512]{3,2,0,1:T(2,128)(2,1)S(1)}, u32[]{:S(2)}, u32[]{:S(2)}) async-start(bf16[1,512,2,512]{3,2,0,1:T(2,128)(2,1)} %copy.51), calls=%async_computation.1 | async-start | bytes 2097152 | tf_op jit(solution)/shard_map/all_to_all | solution.py:58
  313.2 0.5 copy.38
  313.8 22.6 %all-to-all-done.1 = bf16[1,512,2,512]{3,2,0,1:T(2,128)(2,1)S(1)} async-done(((bf16[1,512,2,512]{3,2,0,1:T(2,128)(2,1)}), bf16[1,512,2,512]{3,2,0,1:T(2,128)(2,1)S(1)}, u32[]{:S(2)}, u32[]{:S(2)}) %all-to-all-start.1) | async-done | bytes 1048608 | tf_op jit(solution)/shard_map/all_to_all | solution.py:58
  336.6 0.7 fusion.39
  337.3 0.7 fusion.38
  338.0 0.6 fusion.36
  338.7 2.0 copy.53
  (20 shorter events, 2.0 us)
Async XLA Ops:
  64.1 3.7 %copy-start.1 = (bf16[1,1,512,2,512]{2,4,3,1,0:T(8,128)(2,1)S(1)}, bf16[1,1,512,2,512]{2,4,3,1,0:T(8,128)(2,1)}, u32[]{:S(2)}) copy-start(bf16[1,1,512,2,512]{2,4,3,1,0:T(8,128)(2,1)} %copy.71) | copy-start | bytes 3145732
  70.8 1.5 copy-start
  74.8 3.7 %copy-start.2 = (bf16[1,1,512,2,512]{2,4,3,1,0:T(8,128)(2,1)S(1)}, bf16[1,1,512,2,512]{2,4,3,1,0:T(8,128)(2,1)}, u32[]{:S(2)}) copy-start(bf16[1,1,512,2,512]{2,4,3,1,0:T(8,128)(2,1)} %copy.59) | copy-start | bytes 3145732
  268.5 1.2 copy-start.3
  274.2 3.9 %copy-start.5 = (bf16[512,2,512]{2,0,1:T(8,128)(2,1)S(1)}, bf16[512,2,512]{2,0,1:T(8,128)(2,1)}, u32[]{:S(2)}) copy-start(bf16[512,2,512]{2,0,1:T(8,128)(2,1)} %get-tuple-element.7) | copy-start | bytes 3145732
  274.2 26.6 %all-to-all-start = ((bf16[1,512,2,512]{3,2,0,1:T(2,128)(2,1)}), bf16[1,512,2,512]{3,2,0,1:T(2,128)(2,1)S(1)}, u32[]{:S(2)}, u32[]{:S(2)}) async-start(bf16[1,512,2,512]{3,2,0,1:T(2,128)(2,1)} %copy.46), calls=%async_computation | async-start | bytes 2097152 | tf_op jit(solution)/shard_map/all_to_all | solution.py:58
  304.6 8.6 %copy-start.4 = (bf16[512,2,512]{2,0,1:T(8,128)(2,1)S(1)}, bf16[512,2,512]{2,0,1:T(8,128)(2,1)}, u32[]{:S(2)}) copy-start(bf16[512,2,512]{2,0,1:T(8,128)(2,1)} %get-tuple-element.5) | copy-start | bytes 3145732
  306.7 29.7 %all-to-all-start.1 = ((bf16[1,512,2,512]{3,2,0,1:T(2,128)(2,1)}), bf16[1,512,2,512]{3,2,0,1:T(2,128)(2,1)S(1)}, u32[]{:S(2)}, u32[]{:S(2)}) async-start(bf16[1,512,2,512]{3,2,0,1:T(2,128)(2,1)} %copy.51), calls=%async_computation.1 | async-start | bytes 2097152 | tf_op jit(solution)/shard_map/all_to_all | solution.py:58
where the time goes:
time: 343 us; the launch traced here: 341 us
  blocking collectives  185 us (54%)
  local copies, waits for them, and re-layouts  69.2 us (20%)
  waiting for transfers between devices  43.3 us (13%)
  matrix products  16.1 us (5%)
  starting transfers between devices  10.4 us (3%)
  other arithmetic  8.63 us (3%)
  between operations  7.62 us (2%)
    psum x1, blocking collectives, on_device(): lax.psum((leaf_term(leaves[0][0], leaves[0][1], width), leaf_term(leaves[...  185 us
    all_to_all x2, waiting for transfers between devices, on_device(): lax.all_to_all(absorbed, 'outer', split_axis=1, concat_axis=0, tiled=True)  43.3 us
    unnamed x21, local copies, waits for them, and re-layouts  25.6 us
    all_to_all x2, starting transfers between devices, on_device(): lax.all_to_all(absorbed, 'outer', split_axis=1, concat_axis=0, tiled=True)  10.4 us
    dot_general x4, matrix products, leaf_term(): lax.dot_general(left_leaf.reshape(depth, 2 * row_count), right_leaf.resha...  10.3 us
    slice x1, local copies, waits for them, and re-layouts, on_device(): leaf_left[branch_index]  8.94 us
    slice x1, local copies, waits for them, and re-layouts, on_device(): leaf_right[branch_index]  8.84 us
    dynamic_slice x2, local copies, waits for them, and re-layouts, on_device(): lax.dynamic_index_in_dim(leaf_left[branch_index], chosen, 0, keepdims=False)  8.03 us
  transfers between devices with their start and end apart: 2, of which 2 were waited for; matrix products, arithmetic and copies ran while one was open for 1% of the time, Pallas kernels for 0%

commit v1 on v0

v1 whole, which is shorter than its diff:
```python
import functools

import jax
import jax.numpy as jnp
from jax import lax
from jax.experimental import pallas as pl
from jax.experimental.pallas import tpu as pltpu
from jax.sharding import PartitionSpec as P

ROUNDS = 2
CHUNKS = 4
MESH = pl.DeviceIdType.MESH


def exchange_kernel(n, part, blocks, out, got, acc, outgoing, incoming, a_send, a_recv, r_send, r_recv):
    chunks = part.shape[0]
    steps = n.bit_length() - 1
    me = lax.axis_index("outer")

    barrier = pltpu.get_barrier_semaphore()

    def greet(k, carry):
        pl.semaphore_signal(barrier, inc=1, device_id={"outer": lax.rem(me + k, n)}, device_id_type=MESH)
        return carry

    lax.fori_loop(1, n, greet, 0)
    pl.semaphore_wait(barrier, n - 1)

    bits = [lax.rem(me // (1 << s), 2) for s in range(steps)]
    peers = [me + (1 << s) * (1 - 2 * bits[s]) for s in range(steps)]
    starts = [0]
    gives = []
    for s in range(steps):
        half = n >> (s + 1)
        gives.append(starts[s] + (1 - bits[s]) * half)
        starts.append(starts[s] + bits[s] * half)

    def move(k):
        to = lax.rem(me + k, n)
        return pltpu.make_async_remote_copy(
            src_ref=blocks.at[to], dst_ref=got.at[me], send_sem=a_send.at[k], recv_sem=a_recv.at[k],
            device_id={"outer": to}, device_id_type=MESH)

    def arrival(k):
        origin = lax.rem(me + n - k, n)
        return pltpu.make_async_remote_copy(
            src_ref=blocks.at[origin], dst_ref=got.at[origin], send_sem=a_send.at[k], recv_sem=a_recv.at[k],
            device_id={"outer": origin}, device_id_type=MESH)

    def reduce_copy(c, s):
        half, at = n >> (s + 1), n - (n >> s)
        return pltpu.make_async_remote_copy(
            src_ref=outgoing.at[c, pl.ds(gives[s], half)], dst_ref=incoming.at[c, pl.ds(at, half)],
            send_sem=r_send.at[c, s], recv_sem=r_recv.at[c, s],
            device_id={"outer": peers[s]}, device_id_type=MESH)

    def gather_copy(c, s, first):
        half = n >> (s + 1)
        here = out.at[c, pl.ds(first, half)]
        return pltpu.make_async_remote_copy(
            src_ref=here, dst_ref=here, send_sem=r_send.at[c, 2 * steps - 1 - s], recv_sem=r_recv.at[c, 2 * steps - 1 - s],
            device_id={"outer": peers[s]}, device_id_type=MESH)

    def begin(c, step):
        if step < steps:
            half = n >> (step + 1)
            source = part if step == 0 else acc
            give = pl.ds(gives[step], half)
            outgoing[c, give] = source[c, give].astype(outgoing.dtype)
            reduce_copy(c, step).start()
        else:
            s = 2 * steps - 1 - step
            gather_copy(c, s, starts[s + 1]).start()

    def finish(c, step):
        if step < steps:
            half, at = n >> (step + 1), n - (n >> step)
            reduce_copy(c, step).wait_recv()
            source = part if step == 0 else acc
            keep = pl.ds(starts[step + 1], half)
            total = source[c, keep] + incoming[c, pl.ds(at, half)].astype(jnp.float32)
            if step == steps - 1:
                out[c, keep] = total.astype(out.dtype)
            else:
                acc[c, keep] = total
        else:
            s = 2 * steps - 1 - step
            gather_copy(c, s, gives[s]).wait_recv()

    slots = chunks + 2 * steps
    sent = 1
    for t in range(slots):
        for c in range(chunks):
            step = t - c
            if 1 <= step <= 2 * steps:
                finish(c, step - 1)
            if 0 <= step < 2 * steps:
                begin(c, step)
        upto = min(n, 1 + -(-(n - 1) * (t + 1) // max(1, slots - 3)))

        def launch(k, carry):
            move(k).start()
            return carry

        if upto > sent:
            lax.fori_loop(sent, upto, launch, 0)
            sent = upto
    got[me] = blocks[me]

    def settle(k, carry):
        arrival(k).wait_recv()
        move(k).wait_send()
        return carry

    lax.fori_loop(1, n, settle, 0)
    for c in range(chunks):
        for s in range(steps):
            reduce_copy(c, s).wait_send()
            gather_copy(c, s, starts[s + 1]).wait_send()


def exchange(n, part, blocks, call):
    chunks, steps = part.shape[0], n.bit_length() - 1
    vmem = pl.BlockSpec(memory_space=pltpu.VMEM)
    return pl.pallas_call(
        functools.partial(exchange_kernel, n),
        out_shape=(
            jax.ShapeDtypeStruct(part.shape, jnp.bfloat16),
            jax.ShapeDtypeStruct(blocks.shape, blocks.dtype),
        ),
        in_specs=[vmem, vmem],
        out_specs=(vmem, vmem),
        scratch_shapes=[
            pltpu.VMEM(part.shape, jnp.float32),
            pltpu.VMEM(part.shape, jnp.bfloat16),
            pltpu.VMEM(part.shape, jnp.bfloat16),
            pltpu.SemaphoreType.DMA((n,)),
            pltpu.SemaphoreType.DMA((n,)),
            pltpu.SemaphoreType.DMA((chunks, 2 * steps)),
            pltpu.SemaphoreType.DMA((chunks, 2 * steps)),
        ],
        compiler_params=pltpu.CompilerParams(collective_id=call, has_side_effects=True),
    )(part, blocks)


def leaf_term(left_leaf, right_leaf):
    depth, _, row_count = left_leaf.shape
    width = right_leaf.shape[2]
    product = lax.dot_general(
        left_leaf.reshape(depth, 2 * row_count),
        right_leaf.reshape(depth, 2 * width),
        (((0,), (0,)), ((), ())),
        preferred_element_type=jnp.float32,
    )
    product = product.reshape(2, row_count, 2, width)
    real_part = product[0, :, 0] - product[1, :, 1]
    imag_part = product[0, :, 1] + product[1, :, 0]
    return jnp.stack([real_part, imag_part], axis=0)


def complex_product(left, right, dims):
    def dot(a, b):
        return lax.dot_general(a, b, (dims, ((), ())), preferred_element_type=jnp.float32)

    real_part = dot(left[0], right[0]) - dot(left[1], right[1])
    imag_part = dot(left[0], right[1]) + dot(left[1], right[0])
    return jnp.stack([real_part, imag_part], axis=0).astype(jnp.bfloat16)


def on_device(n, stem_tensor, leaf_left, leaf_right, slice_bits):
    width, columns = stem_tensor.shape[1], stem_tensor.shape[3]
    span = width // n
    state = jnp.transpose(stem_tensor[0], (1, 0, 2))
    parts = []
    for branch_index in range(2 * ROUNDS):
        chosen = slice_bits[branch_index]
        parts.append(
            leaf_term(
                lax.dynamic_index_in_dim(leaf_left[branch_index], chosen, 0, keepdims=False),
                lax.dynamic_index_in_dim(leaf_right[branch_index], chosen, 0, keepdims=False),
            )
        )
    for r in range(ROUNDS):
        part = jnp.stack(parts[2 * r : 2 * r + 2])
        part = part.reshape(CHUNKS, n, -1, columns)
        blocks = jnp.transpose(state.reshape(2, n, span, columns), (1, 0, 2, 3)).reshape(n, 2 * span, columns)
        branches, got = exchange(n, part, blocks, r)
        branches = branches.reshape(2, 2, width, columns)
        regrouped = jnp.transpose(got.reshape(n, 2, span, columns), (1, 0, 2, 3)).reshape(2, width, columns)
        absorbed = complex_product(regrouped, branches[1], ((1,), (0,)))
        state = complex_product(branches[0], absorbed, ((0,), (0,)))
    return jnp.transpose(state, (1, 0, 2))[None]


def solution(mesh):
    return jax.shard_map(
        functools.partial(on_device, mesh.shape["outer"]),
        mesh=mesh,
        in_specs=(
            P(("cuts", "outer"), None, None, None),
            P(None, None, "outer", None, None),
            P(None, None, "outer", None, None),
            P("cuts"),
        ),
        out_specs=P(("cuts", "outer"), None, None, None),
        check_vma=False,
    )
```

time: 343 us -> 220 us (0.64)
  blocking collectives: 185 us -> 0 us
  Pallas kernels: 0 us -> 125 us
  waiting for transfers between devices: 43.3 us -> 0 us
  starting transfers between devices: 10.4 us -> 0 us
  local copies, waits for them, and re-layouts: 69.2 us -> 64.6 us
    psum x1 -> x0, blocking collectives: 185 us -> none  [on_device(): lax.psum((leaf_term(leaves[0][0], leaves[0][1], width), leaf_term(leaves[...]
    pallas_call x0 -> x2, Pallas kernels: none -> 125 us  [exchange(): pl.pallas_call(functools.partial(exchange_kernel, n), out_shape=(jax.Shap...]
    all_to_all x2 -> x0, waiting for transfers between devices: 43.3 us -> none  [on_device(): lax.all_to_all(absorbed, 'outer', split_axis=1, concat_axis=0, tiled=True)]
    all_to_all x2 -> x0, starting transfers between devices: 10.4 us -> none  [on_device(): lax.all_to_all(absorbed, 'outer', split_axis=1, concat_axis=0, tiled=True)]
    another operation x3 -> x0, local copies, waits for them, and re-layouts: 6.23 us -> none  [the longest x2 4.18 us: absorb_columns(): return jnp.stack([real_part, imag_part], axis=1).astype(jnp.bfloat16)]
    dot_general x4, matrix products: 10.3 us -> 6.34 us  [leaf_term(): lax.dot_general(left_leaf.reshape(depth, 2 * row_count), right_leaf.resha...]
    slice x0 -> x4, local copies, waits for them, and re-layouts: none -> 3.62 us  [complex_product(): real_part = dot(left[0], right[0]) - dot(left[1], right[1])]
    dot_general x8 -> x16, matrix products: 5.81 us -> 7.35 us  [dot(): lax.dot_general(a, b, (dims, ((), ())), preferred_element_type=jnp.float32)]
  transfers between devices with their start and end apart: 2 -> 0, of which waited for: 2 -> 0; matrix products, arithmetic and copies ran while one was open for 1% -> 0% of each run, Pallas kernels for 0% -> 0%
where the time goes in v1:
time: 220 us
  Pallas kernels  125 us (57%)
  local copies, waits for them, and re-layouts  64.6 us (29%)
  matrix products  13.7 us (6%)
  other arithmetic  8.6 us (4%)
  between operations  7.86 us (4%)
    pallas_call x2, Pallas kernels, exchange(): pl.pallas_call(functools.partial(exchange_kernel, n), out_shape=(jax.Shap...  125 us
    unnamed x24, local copies, waits for them, and re-layouts  26.1 us
    slice x1, local copies, waits for them, and re-layouts, on_device(): leaf_left[branch_index]  8.43 us
    slice x1, local copies, waits for them, and re-layouts, on_device(): leaf_right[branch_index]  8.43 us
    dot_general x16, matrix products, dot(): lax.dot_general(a, b, (dims, ((), ())), preferred_element_type=jnp.float32)  7.35 us
    dot_general x4, matrix products, leaf_term(): lax.dot_general(left_leaf.reshape(depth, 2 * row_count), right_leaf.resha...  6.34 us
    dynamic_slice x2, local copies, waits for them, and re-layouts, on_device(): lax.dynamic_index_in_dim(leaf_right[branch_index], chosen, 0, keepdims=Fa...  6.04 us
    dynamic_slice x2, local copies, waits for them, and re-layouts, on_device(): lax.dynamic_index_in_dim(leaf_left[branch_index], chosen, 0, keepdims=False)  6.04 us

profile of v1, /device:TPU:1, one launch (start us, length us, event | category | flops | bytes accessed | tf_op | source)
XLA Modules:
  0.0 219.6 jit_solution(1214516644109018870)
XLA Ops:
  0.0 1.5 fusion.36
  9.1 2.4 %copy.17 = bf16[2,16,32,512]{3,2,0,1:T(8,128)(2,1)} copy(bf16[2,16,32,512]{3,0,2,1:T(2,128)(2,1)} %bitcast.215) | data formatting | bytes 2097152 | tf_op jit(solution)/shard_map/reshape | solution.py:186
  11.5 8.4 %fusion.30 = (bf16[1,2,512,2,512]{4,3,2,1,0:T(2,128)(2,1)S(1)}, bf16[1,2,512,2,512]{4,3,2,1,0:T(2,128)(2,1)S(1)}, bf16[1,2,512,2,512]{4,3,2,1,0:T(2,128)(2,1)}, bf16[1,2,512,2,512]{4,3,2,1,0:T(2,128)(2,1)S(1)}) fusion(bf16[4,2,512,2,512]{4,3,2,1,0:T(2,128)(2,1)} %param.5), kind=kLoop, calls=%fused_computation.62 | loop fusion | bytes 16777216 | tf_op jit(solution)/shard_map/slice | solution.py:179
  19.9 2.4 %constant_dynamic-slice_fusion.1 = (bf16[1,1,512,2,512]{4,3,2,1,0:T(2,128)(2,1)}, bf16[1,1,512,2,512]{4,3,2,1,0:T(2,128)(2,1)S(1)}) fusion(bf16[1,2,512,2,512]{4,3,2,1,0:T(2,128)(2,1)S(1)} %get-tuple-element.16, s32[]{:T(128)S(6)} %select_n.20, bf16[1,2,512,2,512]{4,3,2,1,0:T(2,128)(2,1)S(1)} %get-tuple-element.13, s32[]{:T(128)S(6)} %select_n.19), kind=kLoop, calls=%fused_computation.55 | loop fusion | bytes 4194312 | tf_op jit(solution)/shard_map/jit(dynamic_index_in_dim)/dynamic_slice | solution.py:179
  22.3 3.7 %copy.38 = bf16[1,1,512,2,512]{2,4,3,1,0:T(8,128)(2,1)} copy(bf16[1,1,512,2,512]{4,3,2,1,0:T(2,128)(2,1)} %get-tuple-element.49) | data formatting | bytes 2097152
  26.0 2.5 %copy.34 = bf16[1,1,512,2,512]{2,4,3,1,0:T(8,128)(2,1)} copy(bf16[1,1,512,2,512]{4,3,2,1,0:T(2,128)(2,1)S(1)} %get-tuple-element.50) | data formatting | bytes 2097152
  28.5 3.6 %constant_dynamic-slice_fusion.5 = (bf16[1,1,512,2,512]{4,3,2,1,0:T(2,128)(2,1)}, bf16[1,1,512,2,512]{4,3,2,1,0:T(2,128)(2,1)S(1)}) fusion(bf16[1,2,512,2,512]{4,3,2,1,0:T(2,128)(2,1)S(1)} %get-tuple-element.14, s32[]{:T(128)S(6)} %select_n.18, bf16[1,2,512,2,512]{4,3,2,1,0:T(2,128)(2,1)} %get-tuple-element.15, s32[]{:T(128)S(6)} %select_n.17), kind=kLoop, calls=%fused_computation.59 | loop fusion | bytes 4194312 | tf_op jit(solution)/shard_map/jit(dynamic_index_in_dim)/dynamic_slice | solution.py:179
  32.1 3.7 %copy.30 = bf16[1,1,512,2,512]{2,4,3,1,0:T(8,128)(2,1)} copy(bf16[1,1,512,2,512]{4,3,2,1,0:T(2,128)(2,1)} %get-tuple-element.51) | data formatting | bytes 2097152
  35.8 2.5 %copy.26 = bf16[1,1,512,2,512]{2,4,3,1,0:T(8,128)(2,1)} copy(bf16[1,1,512,2,512]{4,3,2,1,0:T(2,128)(2,1)S(1)} %get-tuple-element.52) | data formatting | bytes 2097152
  38.3 8.4 %fusion.31 = (bf16[1,2,512,2,512]{4,3,2,1,0:T(2,128)(2,1)S(1)}, bf16[1,2,512,2,512]{4,3,2,1,0:T(2,128)(2,1)S(1)}, bf16[1,2,512,2,512]{4,3,2,1,0:T(2,128)(2,1)}, bf16[1,2,512,2,512]{4,3,2,1,0:T(2,128)(2,1)S(1)}) fusion(bf16[4,2,512,2,512]{4,3,2,1,0:T(2,128)(2,1)} %param.6), kind=kLoop, calls=%fused_computation.63 | loop fusion | bytes 16777216 | tf_op jit(solution)/shard_map/slice | solution.py:180
  46.7 2.4 %constant_dynamic-slice_fusion = (bf16[1,1,512,2,512]{4,3,2,1,0:T(2,128)(2,1)}, bf16[1,1,512,2,512]{4,3,2,1,0:T(2,128)(2,1)S(1)}) fusion(bf16[1,2,512,2,512]{4,3,2,1,0:T(2,128)(2,1)S(1)} %get-tuple-element.20, s32[]{:T(128)S(6)} %select_n.20, bf16[1,2,512,2,512]{4,3,2,1,0:T(2,128)(2,1)S(1)} %get-tuple-element.17, s32[]{:T(128)S(6)} %select_n.19), kind=kLoop, calls=%fused_computation.54 | loop fusion | bytes 4194312 | tf_op jit(solution)/shard_map/jit(dynamic_index_in_dim)/dynamic_slice | solution.py:180
  49.1 3.7 %copy.40 = bf16[1,1,512,2,512]{2,4,3,1,0:T(8,128)(2,1)} copy(bf16[1,1,512,2,512]{4,3,2,1,0:T(2,128)(2,1)} %get-tuple-element.45) | data formatting | bytes 2097152
  52.8 2.5 %copy.36 = bf16[1,1,512,2,512]{2,4,3,1,0:T(8,128)(2,1)} copy(bf16[1,1,512,2,512]{4,3,2,1,0:T(2,128)(2,1)S(1)} %get-tuple-element.46) | data formatting | bytes 2097152
  55.3 3.6 %constant_dynamic-slice_fusion.4 = (bf16[1,1,512,2,512]{4,3,2,1,0:T(2,128)(2,1)}, bf16[1,1,512,2,512]{4,3,2,1,0:T(2,128)(2,1)S(1)}) fusion(bf16[1,2,512,2,512]{4,3,2,1,0:T(2,128)(2,1)S(1)} %get-tuple-element.18, s32[]{:T(128)S(6)} %select_n.18, bf16[1,2,512,2,512]{4,3,2,1,0:T(2,128)(2,1)} %get-tuple-element.19, s32[]{:T(128)S(6)} %select_n.17), kind=kLoop, calls=%fused_computation.58 | loop fusion | bytes 4194312 | tf_op jit(solution)/shard_map/jit(dynamic_index_in_dim)/dynamic_slice | solution.py:180
  59.0 2.5 %copy.32 = bf16[1,1,512,2,512]{2,4,3,1,0:T(8,128)(2,1)S(1)} copy(bf16[1,1,512,2,512]{4,3,2,1,0:T(2,128)(2,1)} %get-tuple-element.47) | data formatting | bytes 2097152
  61.5 2.5 %copy.28 = bf16[1,1,512,2,512]{2,4,3,1,0:T(8,128)(2,1)} copy(bf16[1,1,512,2,512]{4,3,2,1,0:T(2,128)(2,1)S(1)} %get-tuple-element.48) | data formatting | bytes 2097152
  64.0 2.5 %fusion.27 = f32[2,512,2,512]{3,1,2,0:T(8,128)S(1)} fusion(bf16[1,1,512,2,512]{2,4,3,1,0:T(8,128)(2,1)} %copy.28, bf16[1,1,512,2,512]{2,4,3,1,0:T(8,128)(2,1)S(1)} %copy-done.5), kind=kOutput, calls=%fused_computation.51 | convolution fusion | flops 1073741824 | bytes 6291456 | tf_op jit(solution)/shard_map/dot_general | solution.py:149
  66.5 0.5 fusion.17
  67.2 1.0 copy-done.3
  68.2 1.3 fusion.24
  69.5 0.5 fusion.15
  70.2 2.4 %pad_maximum_fusion = f32[2,2,512,512]{3,2,1,0:T(8,128)} fusion(f32[1,2,512,512]{3,2,1,0:T(8,128)S(1)} %maximum_bitcast_fusion.1, f32[1,2,512,512]{3,2,1,0:T(8,128)S(1)} %maximum_bitcast_fusion), kind=kLoop, calls=%fused_computation | loop fusion | flops 1048576 | bytes 8388608 | tf_op jit(solution)/shard_map/stack | solution.py:184
  72.6 1.3 fusion.21
  73.9 0.5 fusion.13
  74.6 1.0 copy-done
  75.9 1.3 fusion.18
  77.2 0.5 fusion.11
  77.8 2.4 %pad_maximum_fusion.1 = f32[2,2,512,512]{3,2,1,0:T(8,128)} fusion(f32[1,2,512,512]{3,2,1,0:T(8,128)S(1)} %maximum_bitcast_fusion.3, f32[1,2,512,512]{3,2,1,0:T(8,128)S(1)} %maximum_bitcast_fusion.2), kind=kLoop, calls=%fused_computation.1 | loop fusion | flops 1048576 | bytes 8388608 | tf_op jit(solution)/shard_map/stack | solution.py:184
  80.3 62.4 %shard_map.46 = (bf16[4,16,32,512]{3,2,1,0:T(8,128)(2,1)}, bf16[16,64,512]{2,1,0:T(8,128)(2,1)}) custom-call(f32[4,16,32,512]{3,2,1,0:T(8,128)} %bitcast.186, bf16[16,64,512]{2,1,0:T(8,128)(2,1)} %bitcast.211), custom_call_target="tpu_custom_call" | custom-call | tf_op jit(solution)/shard_map/pallas_call | solution.py:125
  142.7 1.7 fusion.33
  144.6 0.4 fusion.39
  145.1 0.4 fusion.1
  146.0 0.4 fusion
  146.4 0.5 fusion.38
  146.9 0.5 fusion.2
  147.4 0.5 fusion.40
  147.9 0.5 fusion.3
  148.3 1.1 pad_maximum_fusion.2
  149.4 62.4 %shard_map.47 = (bf16[4,16,32,512]{3,2,1,0:T(8,128)(2,1)}, bf16[16,64,512]{2,1,0:T(8,128)(2,1)}) custom-call(f32[4,16,32,512]{3,2,1,0:T(8,128)} %bitcast.185, bf16[16,64,512]{2,1,0:T(8,128)(2,1)} %bitcast.212), custom_call_target="tpu_custom_call" | custom-call | tf_op jit(solution)/shard_map/pallas_call | solution.py:125
  211.8 1.7 fusion.32
  213.7 0.4 fusion.43
  214.1 0.4 fusion.5
  215.0 0.4 fusion.4
  215.5 0.5 fusion.42
  216.0 0.5 fusion.9
  216.4 0.5 fusion.44
  216.9 0.5 fusion.8
  217.5 2.0 copy.20
  (23 shorter events, 2.3 us)
Async XLA Ops:
  59.0 5.0 %copy-start.5 = (bf16[1,1,512,2,512]{2,4,3,1,0:T(8,128)(2,1)S(1)}, bf16[1,1,512,2,512]{2,4,3,1,0:T(8,128)(2,1)}, u32[]{:S(2)}) copy-start(bf16[1,1,512,2,512]{2,4,3,1,0:T(8,128)(2,1)} %copy.26) | copy-start | bytes 3145732
  67.0 1.2 copy-start.3
  70.2 2.4 %copy-start.1 = (bf16[1,1,512,2,512]{2,4,3,1,0:T(8,128)(2,1)S(1)}, bf16[1,1,512,2,512]{2,4,3,1,0:T(8,128)(2,1)}, u32[]{:S(2)}) copy-start(bf16[1,1,512,2,512]{2,4,3,1,0:T(8,128)(2,1)} %copy.34) | copy-start | bytes 3145732
  70.2 2.4 %copy-start.4 = (bf16[1,1,512,2,512]{2,4,3,1,0:T(8,128)(2,1)S(1)}, bf16[1,1,512,2,512]{2,4,3,1,0:T(8,128)(2,1)}, u32[]{:S(2)}) copy-start(bf16[1,1,512,2,512]{2,4,3,1,0:T(8,128)(2,1)} %copy.36) | copy-start | bytes 3145732
  74.4 1.2 copy-start
  74.4 1.5 copy-start.2
  142.7 1.9 copy-start.6
  211.8 1.9 copy-start.7

commit v2 on v1

--- a/solution.py
+++ b/solution.py
@@ -143,19 +143,39 @@
     )(part, blocks)
 
 
-def leaf_term(left_leaf, right_leaf):
-    depth, _, row_count = left_leaf.shape
-    width = right_leaf.shape[2]
-    product = lax.dot_general(
-        left_leaf.reshape(depth, 2 * row_count),
-        right_leaf.reshape(depth, 2 * width),
-        (((0,), (0,)), ((), ())),
-        preferred_element_type=jnp.float32,
-    )
-    product = product.reshape(2, row_count, 2, width)
-    real_part = product[0, :, 0] - product[1, :, 1]
-    imag_part = product[0, :, 1] + product[1, :, 0]
-    return jnp.stack([real_part, imag_part], axis=0)
+def leaf_kernel(bits, left_ref, right_ref, out_ref):
+    depth, row_count = left_ref.shape[2], left_ref.shape[4]
+    width = right_ref.shape[4]
+    left = left_ref[0, 0].reshape(2 * depth, row_count)
+    right = right_ref[0, 0].reshape(2 * depth, width).astype(jnp.float32)
+    even = lax.rem(lax.broadcasted_iota(jnp.int32, right.shape, 0), 2) == 0
+    signed = jnp.where(even, right, -right).astype(jnp.bfloat16)
+    swapped = jnp.where(even, pltpu.roll(right, 2 * depth - 1, 0), pltpu.roll(right, 1, 0)).astype(jnp.bfloat16)
+    dims = (((0,), (0,)), ((), ()))
+    out_ref[0, 0] = lax.dot_general(left, signed, dims, preferred_element_type=jnp.float32)
+    out_ref[0, 1] = lax.dot_general(left, swapped, dims, preferred_element_type=jnp.float32)
+
+
+def leaf_terms(bits, leaf_left, leaf_right, first):
+    _, _, depth, _, row_count = leaf_left.shape
+    width = leaf_right.shape[4]
+
+    def chosen(j, chosen_bits):
+        return (first + j, chosen_bits[first + j], 0, 0, 0)
+
+    return pl.pallas_call(
+        leaf_kernel,
+        out_shape=jax.ShapeDtypeStruct((2, 2, row_count, width), jnp.float32),
+        grid_spec=pltpu.PrefetchScalarGridSpec(
+            num_scalar_prefetch=1,
+            grid=(2,),
+            in_specs=[
+                pl.BlockSpec((1, 1, depth, 2, row_count), chosen),
+                pl.BlockSpec((1, 1, depth, 2, width), chosen),
+            ],
+            out_specs=pl.BlockSpec((1, 2, row_count, width), lambda j, chosen_bits: (j, 0, 0, 0)),
+        ),
+    )(bits, leaf_left, leaf_right)
 
 
 def complex_product(left, right, dims):
@@ -171,18 +191,8 @@
     width, columns = stem_tensor.shape[1], stem_tensor.shape[3]
     span = width // n
     state = jnp.transpose(stem_tensor[0], (1, 0, 2))
-    parts = []
-    for branch_index in range(2 * ROUNDS):
-        chosen = slice_bits[branch_index]
-        parts.append(
-            leaf_term(
-                lax.dynamic_index_in_dim(leaf_left[branch_index], chosen, 0, keepdims=False),
-                lax.dynamic_index_in_dim(leaf_right[branch_index], chosen, 0, keepdims=False),
-            )
-        )
     for r in range(ROUNDS):
-        part = jnp.stack(parts[2 * r : 2 * r + 2])
-        part = part.reshape(CHUNKS, n, -1, columns)
+        part = leaf_terms(slice_bits, leaf_left, leaf_right, 2 * r).reshape(CHUNKS, n, -1, columns)
         blocks = jnp.transpose(state.reshape(2, n, span, columns), (1, 0, 2, 3)).reshape(n, 2 * span, columns)
         branches, got = exchange(n, part, blocks, r)
         branches = branches.reshape(2, 2, width, columns)

time: 220 us -> 157 us (0.71)
  local copies, waits for them, and re-layouts: 64.6 us -> 8.29 us
  Pallas kernels: 125 us -> 139 us
  between operations: 7.86 us -> 0.12 us
  other arithmetic: 8.6 us -> 1.16 us
  matrix products: 13.7 us -> 7.35 us
    unnamed x24 -> x4, local copies, waits for them, and re-layouts: 26.1 us -> 0.2 us
    slice x3 -> x0, local copies, waits for them, and re-layouts: 18.3 us -> none  [the longest x1 8.43 us: on_device(): leaf_left[branch_index]]
    pallas_call x0 -> x2, Pallas kernels: none -> 14.7 us  [leaf_terms(): pl.pallas_call(leaf_kernel, out_shape=jax.ShapeDtypeStruct((2, 2, row_cou...]
    dynamic_slice x4 -> x0, local copies, waits for them, and re-layouts: 12.1 us -> none  [the longest x2 6.04 us: on_device(): lax.dynamic_index_in_dim(leaf_right[branch_index], chosen, 0, keepdims=Fa...]
    dot_general x4 -> x0, matrix products: 6.34 us -> none  [leaf_term(): lax.dot_general(left_leaf.reshape(depth, 2 * row_count), right_leaf.resha...]
    another operation x6 -> x0, other arithmetic: 5.52 us -> none  [on_device(): part = jnp.stack(parts[2 * r:2 * r + 2])]
where the time goes in v2:
time: 157 us; the launch traced here: 156 us
  Pallas kernels  139 us (89%)
  local copies, waits for them, and re-layouts  8.29 us (5%)
  matrix products  7.35 us (5%)
    pallas_call x2, Pallas kernels, exchange(): pl.pallas_call(functools.partial(exchange_kernel, n), out_shape=(jax.Shap...  125 us
    pallas_call x2, Pallas kernels, leaf_terms(): pl.pallas_call(leaf_kernel, out_shape=jax.ShapeDtypeStruct((2, 2, row_cou...  14.7 us
    dot_general x16, matrix products, dot(): lax.dot_general(a, b, (dims, ((), ())), preferred_element_type=jnp.float32)  7.35 us
    slice x4, local copies, waits for them, and re-layouts, complex_product(): real_part = dot(left[0], right[0]) - dot(left[1], right[1])  3.62 us

profile of v2, /device:TPU:1, one launch (start us, length us, event | category | flops | bytes accessed | tf_op | source)
XLA Modules:
  0.0 156.4 jit_solution(5326858222374705844)
XLA Ops:
  0.0 2.4 %copy.5 = bf16[2,16,32,512]{3,2,0,1:T(8,128)(2,1)} copy(bf16[2,16,32,512]{3,0,2,1:T(2,128)(2,1)} %bitcast.107) | data formatting | bytes 2097152 | tf_op jit(solution)/shard_map/reshape | solution.py:196
  2.4 7.3 %shard_map.47 = f32[2,2,512,512]{3,2,1,0:T(8,128)} custom-call(s32[4]{0:T(128)} %bits.3, bf16[4,2,512,2,512]{4,3,2,1,0:T(2,128)(2,1)} %left_ref.3, bf16[4,2,512,2,512]{4,3,2,1,0:T(2,128)(2,1)} %right_ref.3), custom_call_target="tpu_custom_call" | custom-call | tf_op jit(solution)/shard_map/pallas_call | solution.py:166
  9.8 62.4 %shard_map.48 = (bf16[4,16,32,512]{3,2,1,0:T(8,128)(2,1)}, bf16[16,64,512]{2,1,0:T(8,128)(2,1)}) custom-call(f32[4,16,32,512]{3,2,1,0:T(8,128)} %bitcast.77, bf16[16,64,512]{2,1,0:T(8,128)(2,1)} %bitcast.104), custom_call_target="tpu_custom_call" | custom-call | tf_op jit(solution)/shard_map/pallas_call | solution.py:125
  72.2 0.0 copy-start
  72.2 1.7 %fusion.11 = (bf16[1,16,32,512]{3,2,1,0:T(8,128)(2,1)S(1)}, bf16[1,16,32,512]{3,2,1,0:T(8,128)(2,1)S(1)}, bf16[1,16,32,512]{3,2,1,0:T(8,128)(2,1)S(1)}, bf16[1,16,32,512]{3,2,1,0:T(8,128)(2,1)S(1)}) fusion(bf16[4,16,32,512]{3,2,1,0:T(8,128)(2,1)} %get-tuple-element.9), kind=kLoop, calls=%fused_computation.21 | loop fusion | bytes 4194304 | tf_op jit(solution)/shard_map/slice | solution.py:185
  73.9 0.1 copy-done
  74.0 0.1 fusion.13
  74.1 0.4 fusion.16
  74.6 0.4 fusion.1
  75.0 0.4 fusion.14
  75.5 0.4 fusion
  75.9 0.5 fusion.15
  76.4 0.5 fusion.2
  76.9 0.5 fusion.17
  77.3 0.5 fusion.3
  77.8 1.1 pad_maximum_fusion
  78.9 7.3 %shard_map.46 = f32[2,2,512,512]{3,2,1,0:T(8,128)} custom-call(s32[4]{0:T(128)} %bits.3, bf16[4,2,512,2,512]{4,3,2,1,0:T(2,128)(2,1)} %left_ref.3, bf16[4,2,512,2,512]{4,3,2,1,0:T(2,128)(2,1)} %right_ref.3), custom_call_target="tpu_custom_call" | custom-call | tf_op jit(solution)/shard_map/pallas_call | solution.py:166
  86.2 62.4 %shard_map.49 = (bf16[4,16,32,512]{3,2,1,0:T(8,128)(2,1)}, bf16[16,64,512]{2,1,0:T(8,128)(2,1)}) custom-call(f32[4,16,32,512]{3,2,1,0:T(8,128)} %bitcast.78, bf16[16,64,512]{2,1,0:T(8,128)(2,1)} %bitcast.103), custom_call_target="tpu_custom_call" | custom-call | tf_op jit(solution)/shard_map/pallas_call | solution.py:125
  148.6 0.0 copy-start.1
  148.6 1.7 %fusion.10 = (bf16[1,16,32,512]{3,2,1,0:T(8,128)(2,1)S(1)}, bf16[1,16,32,512]{3,2,1,0:T(8,128)(2,1)S(1)}, bf16[1,16,32,512]{3,2,1,0:T(8,128)(2,1)S(1)}, bf16[1,16,32,512]{3,2,1,0:T(8,128)(2,1)S(1)}) fusion(bf16[4,16,32,512]{3,2,1,0:T(8,128)(2,1)} %get-tuple-element.11), kind=kLoop, calls=%fused_computation.20 | loop fusion | bytes 4194304 | tf_op jit(solution)/shard_map/slice | solution.py:185
  150.4 0.1 copy-done.1
  150.5 0.1 fusion.12
  150.5 0.4 fusion.20
  151.0 0.4 fusion.5
  151.4 0.4 fusion.18
  151.9 0.4 fusion.4
  152.3 0.5 fusion.19
  152.8 0.5 fusion.9
  153.3 0.5 fusion.21
  153.8 0.5 fusion.8
  154.2 0.1 maximum_bitcast_fusion
  154.3 2.0 %copy.8 = bf16[1,512,2,512]{3,2,1,0:T(2,128)(2,1)} copy(bf16[1,512,2,512]{3,1,2,0:T(8,128)(2,1)S(1)} %maximum_bitcast_fusion) | data formatting | bytes 2097152 | tf_op jit(solution)/shard_map/broadcast_in_dim | solution.py:202
Async XLA Ops:
  72.2 1.9 %copy-start = (bf16[16,64,512]{2,1,0:T(8,128)(2,1)S(1)}, bf16[16,64,512]{2,1,0:T(8,128)(2,1)}, u32[]{:S(2)}) copy-start(bf16[16,64,512]{2,1,0:T(8,128)(2,1)} %get-tuple-element.10) | copy-start | bytes 3145732
  148.6 1.9 %copy-start.1 = (bf16[16,64,512]{2,1,0:T(8,128)(2,1)S(1)}, bf16[16,64,512]{2,1,0:T(8,128)(2,1)}, u32[]{:S(2)}) copy-start(bf16[16,64,512]{2,1,0:T(8,128)(2,1)} %get-tuple-element.12) | copy-start | bytes 3145732

commit v3 on v2

v3 whole, which is shorter than its diff:
```python
import functools

import jax
import jax.numpy as jnp
from jax import lax
from jax.experimental import pallas as pl
from jax.experimental.pallas import tpu as pltpu
from jax.sharding import PartitionSpec as P

ROUNDS = 2
PLANES = 4
TILES = 4
LAG = 2
EARLY = 4
SPREAD = 0.8
UNITS = 2
MESH = pl.DeviceIdType.MESH


def network_kernel(
    n, part0, part1, blocks0, out, acc, outgoing, incoming, branch, got0, got1, blocks1, absorbed,
    a_send, a_recv, r_send, r_recv,
):
    planes = part0.shape[0]
    chunks = 2 * planes
    span, columns = part0.shape[2], part0.shape[3]
    width = n * span
    steps = n.bit_length() - 1
    tiles = TILES
    group = n // tiles
    me = lax.axis_index("outer")
    high, low = me // group, lax.rem(me, group)

    barrier = pltpu.get_barrier_semaphore()

    def greet(k, carry):
        pl.semaphore_signal(barrier, inc=1, device_id={"outer": lax.rem(me + k, n)}, device_id_type=MESH)
        return carry

    lax.fori_loop(1, n, greet, 0)
    pl.semaphore_wait(barrier, n - 1)

    bits = [lax.rem(me // (1 << s), 2) for s in range(steps)]
    peers = [me + (1 << s) * (1 - 2 * bits[s]) for s in range(steps)]
    starts = [0]
    gives = []
    for s in range(steps):
        half = n >> (s + 1)
        gives.append(starts[s] + (1 - bits[s]) * half)
        starts.append(starts[s] + bits[s] * half)

    def copy_to(r, i, j):
        to = lax.rem(high + i, tiles) * group + lax.rem(low + j, group)
        k = i * group + j
        blocks, got = ((blocks0, got0), (blocks1, got1))[r]
        return pltpu.make_async_remote_copy(
            src_ref=blocks.at[to], dst_ref=got.at[me], send_sem=a_send.at[r, k], recv_sem=a_recv.at[r, k],
            device_id={"outer": to}, device_id_type=MESH)

    def copy_from(r, i, j):
        origin = lax.rem(high + tiles - i, tiles) * group + lax.rem(low + group - j, group)
        k = i * group + j
        blocks, got = ((blocks0, got0), (blocks1, got1))[r]
        return pltpu.make_async_remote_copy(
            src_ref=blocks.at[origin], dst_ref=got.at[origin], send_sem=a_send.at[r, k], recv_sem=a_recv.at[r, k],
            device_id={"outer": origin}, device_id_type=MESH)

    def over(i, act):
        def one(j, carry):
            act(i, j)
            return carry

        lax.fori_loop(1 if i == 0 else 0, group, one, 0)

    def source(c, step):
        if step:
            return acc, c
        return (part0, c) if c < planes else (part1, c - planes)

    def reduce_copy(c, s):
        half, at = n >> (s + 1), n - (n >> s)
        return pltpu.make_async_remote_copy(
            src_ref=outgoing.at[c, pl.ds(gives[s], half)], dst_ref=incoming.at[c, pl.ds(at, half)],
            send_sem=r_send.at[c, s], recv_sem=r_recv.at[c, s],
            device_id={"outer": peers[s]}, device_id_type=MESH)

    def gather_copy(c, s, first):
        here = branch.at[c, pl.ds(first, n >> (s + 1))]
        return pltpu.make_async_remote_copy(
            src_ref=here, dst_ref=here, send_sem=r_send.at[c, 2 * steps - 1 - s], recv_sem=r_recv.at[c, 2 * steps - 1 - s],
            device_id={"outer": peers[s]}, device_id_type=MESH)

    def begin(c, step):
        if step < steps:
            give = pl.ds(gives[step], n >> (step + 1))
            ref, at = source(c, step)
            outgoing[c, give] = ref[at, give].astype(outgoing.dtype)
            reduce_copy(c, step).start()
        else:
            s = 2 * steps - 1 - step
            gather_copy(c, s, starts[s + 1]).start()

    def finish(c, step):
        if step < steps:
            half, at = n >> (step + 1), n - (n >> step)
            reduce_copy(c, step).wait_recv()
            keep = pl.ds(starts[step + 1], half)
            ref, own = source(c, step)
            total = ref[own, keep] + incoming[c, pl.ds(at, half)].astype(jnp.float32)
            if step == steps - 1:
                branch[c, keep] = total.astype(branch.dtype)
            else:
                acc[c, keep] = total
        else:
            s = 2 * steps - 1 - step
            gather_copy(c, s, gives[s]).wait_recv()

    def dot(a, b):
        return jnp.dot(a, b, preferred_element_type=jnp.float32)

    def absorb(r, i):
        got = (got0, got1)[r]
        over(i, lambda i, j: copy_from(r, i, j).wait_recv())
        here = pl.ds(lax.rem(high + tiles - i, tiles) * group, group)
        entries = got[here].reshape(group * 2 * span, columns)
        first = r * planes
        by_real = dot(entries, branch[first + 2].reshape(width, columns)).reshape(group, 2, span, columns)
        by_imag = dot(entries, branch[first + 3].reshape(width, columns)).reshape(group, 2, span, columns)
        absorbed[0, here] = (by_real[:, 0] - by_imag[:, 1]).astype(absorbed.dtype)
        absorbed[1, here] = (by_imag[:, 0] + by_real[:, 1]).astype(absorbed.dtype)

    def contract(r, where):
        here = pl.ds(where * group, group)
        first = r * planes
        p_real = branch[first, here].reshape(group * span, width)
        p_imag = branch[first + 1, here].reshape(group * span, width)
        a_real, a_imag = absorbed[0].reshape(width, columns), absorbed[1].reshape(width, columns)
        real_part = (dot(p_real, a_real) - dot(p_imag, a_imag)).astype(jnp.bfloat16)
        imag_part = (dot(p_real, a_imag) + dot(p_imag, a_real)).astype(jnp.bfloat16)
        return here, real_part.reshape(group, span, columns), imag_part.reshape(group, span, columns)

    def renew(i):
        here, real_part, imag_part = contract(0, lax.rem(high + i, tiles))
        blocks1[here, 0:span] = real_part
        blocks1[here, span : 2 * span] = imag_part
        if i == 0:
            got1[me] = blocks1[me]
        over(i, lambda i, j: copy_to(1, i, j).start())

    got0[me] = blocks0[me]
    order = [2, 1, 3, 0]
    sends = [(i, j) for i in order for j in range(group) if i or j]
    ready = planes - 1 + 2 * steps * LAG
    entry = [c if c < planes else ready - EARLY + c - planes for c in range(chunks)]
    work = [functools.partial(absorb, 0, i) for i in order] + [functools.partial(renew, i) for i in order]
    unsent = list(order)
    total_slots = entry[-1] + 2 * steps * LAG + 1
    for t in range(total_slots):
        for c in range(chunks):
            if t < entry[c] or (t - entry[c]) % LAG:
                continue
            step = (t - entry[c]) // LAG
            if 1 <= step <= 2 * steps:
                finish(c, step - 1)
            if step < 2 * steps:
                begin(c, step)
        if unsent and t % max(1, int(ready * SPREAD) // tiles) == 0:
            over(unsent.pop(0), lambda i, j: copy_to(0, i, j).start())
        if t >= ready:
            assert not unsent
            for job in work[:UNITS]:
                job()
            work = work[UNITS:]
    assert not work

    for i in order:
        absorb(1, i)
    for where in range(tiles):
        here, real_part, imag_part = contract(1, where)
        out[0, here] = real_part
        out[1, here] = imag_part

    for r in range(2):
        for i in order:
            over(i, lambda i, j: copy_to(r, i, j).wait_send())
    for c in range(chunks):
        for s in range(steps):
            reduce_copy(c, s).wait_send()
            gather_copy(c, s, starts[s + 1]).wait_send()


def contract_network(n, part0, part1, blocks):
    planes, _, span, columns = part0.shape
    steps = n.bit_length() - 1
    both = (2 * planes,) + part0.shape[1:]
    vmem = pl.BlockSpec(memory_space=pltpu.VMEM)
    return pl.pallas_call(
        functools.partial(network_kernel, n),
        out_shape=jax.ShapeDtypeStruct((2, n, span, columns), jnp.bfloat16),
        in_specs=[vmem, vmem, vmem],
        out_specs=vmem,
        scratch_shapes=[
            pltpu.VMEM(both, jnp.float32),
            pltpu.VMEM(both, jnp.bfloat16),
            pltpu.VMEM(both, jnp.bfloat16),
            pltpu.VMEM(both, jnp.bfloat16),
            pltpu.VMEM(blocks.shape, jnp.bfloat16),
            pltpu.VMEM(blocks.shape, jnp.bfloat16),
            pltpu.VMEM(blocks.shape, jnp.bfloat16),
            pltpu.VMEM((2, n, span, columns), jnp.bfloat16),
            pltpu.SemaphoreType.DMA((2, n)),
            pltpu.SemaphoreType.DMA((2, n)),
            pltpu.SemaphoreType.DMA((2 * planes, 2 * steps)),
            pltpu.SemaphoreType.DMA((2 * planes, 2 * steps)),
        ],
        compiler_params=pltpu.CompilerParams(collective_id=0, has_side_effects=True),
    )(part0, part1, blocks)


def leaf_kernel(bits, left_ref, right_ref, out_ref):
    depth, row_count = left_ref.shape[2], left_ref.shape[4]
    width = right_ref.shape[4]
    left = left_ref[0, 0].reshape(2 * depth, row_count)
    right = right_ref[0, 0].reshape(2 * depth, width).astype(jnp.float32)
    even = lax.rem(lax.broadcasted_iota(jnp.int32, right.shape, 0), 2) == 0
    signed = jnp.where(even, right, -right).astype(jnp.bfloat16)
    swapped = jnp.where(even, pltpu.roll(right, 2 * depth - 1, 0), pltpu.roll(right, 1, 0)).astype(jnp.bfloat16)
    def product(a, b):
        return lax.dot_general(a, b, (((0,), (0,)), ((), ())), preferred_element_type=jnp.float32)

    @pl.when(pl.program_id(0) == 0)
    def _():
        out_ref[0, 0] = product(signed, left)
        out_ref[0, 1] = product(swapped, left)

    @pl.when(pl.program_id(0) != 0)
    def _():
        out_ref[0, 0] = product(left, signed)
        out_ref[0, 1] = product(left, swapped)


def leaf_terms(bits, leaf_left, leaf_right, first):
    _, _, depth, _, row_count = leaf_left.shape
    width = leaf_right.shape[4]

    def chosen(j, chosen_bits):
        return (first + j, chosen_bits[first + j], 0, 0, 0)

    return pl.pallas_call(
        leaf_kernel,
        out_shape=jax.ShapeDtypeStruct((2, 2, row_count, width), jnp.float32),
        grid_spec=pltpu.PrefetchScalarGridSpec(
            num_scalar_prefetch=1,
            grid=(2,),
            in_specs=[
                pl.BlockSpec((1, 1, depth, 2, row_count), chosen),
                pl.BlockSpec((1, 1, depth, 2, width), chosen),
            ],
            out_specs=pl.BlockSpec((1, 2, row_count, width), lambda j, chosen_bits: (j, 0, 0, 0)),
        ),
    )(bits, leaf_left, leaf_right)


def on_device(n, stem_tensor, leaf_left, leaf_right, slice_bits):
    width, columns = stem_tensor.shape[1], stem_tensor.shape[3]
    span = width // n
    blocks = jnp.transpose(stem_tensor.reshape(n, span, 2, columns), (0, 2, 1, 3)).reshape(n, 2 * span, columns)
    parts = [
        leaf_terms(slice_bits, leaf_left, leaf_right, 2 * r).reshape(PLANES, n, span, columns) for r in range(ROUNDS)
    ]
    state = contract_network(n, *parts, blocks).reshape(2, width, columns)
    return jnp.transpose(state, (1, 0, 2))[None]


def solution(mesh):
    return jax.shard_map(
        functools.partial(on_device, mesh.shape["outer"]),
        mesh=mesh,
        in_specs=(
            P(("cuts", "outer"), None, None, None),
            P(None, None, "outer", None, None),
            P(None, None, "outer", None, None),
            P("cuts"),
        ),
        out_specs=P(("cuts", "outer"), None, None, None),
        check_vma=False,
    )
```

time: 157 us -> 148 us (0.943)
  matrix products: 7.35 us -> 0 us
  Pallas kernels: 139 us -> 142 us
  local copies, waits for them, and re-layouts: 8.29 us -> 5.69 us
    dot_general x16 -> x0, matrix products: 7.35 us -> none  [dot(): lax.dot_general(a, b, (dims, ((), ())), preferred_element_type=jnp.float32)]
    pallas_call x2, Pallas kernels: 14.7 us -> 20.3 us  [leaf_terms(): pl.pallas_call(leaf_kernel, out_shape=jax.ShapeDtypeStruct((2, 2, row_cou...]
    slice x4 -> x0, local copies, waits for them, and re-layouts: 3.62 us -> none  [complex_product(): real_part = dot(left[0], right[0]) - dot(left[1], right[1])]
    reshape x1 -> x2, local copies, waits for them, and re-layouts: 2.42 us -> 5.69 us  [the longest x1 3.27 us: on_device(): state = contract_network(n, *parts, blocks).reshape(2, width, columns)]
    pallas_call x2 -> x1, Pallas kernels: 125 us -> 122 us  [contract_network(): pl.pallas_call(functools.partial(network_kernel, n), out_shape=jax.ShapeD...]
    broadcast_in_dim x1 -> x0, local copies, waits for them, and re-layouts: 2.05 us -> none  [on_device(): return jnp.transpose(state, (1, 0, 2))[None]]
where the time goes in v3:
time: 148 us
  Pallas kernels  142 us (96%)
  local copies, waits for them, and re-layouts  5.69 us (4%)
    pallas_call x1, Pallas kernels, contract_network(): pl.pallas_call(functools.partial(network_kernel, n), out_shape=jax.ShapeD...  122 us
    pallas_call x2, Pallas kernels, leaf_terms(): pl.pallas_call(leaf_kernel, out_shape=jax.ShapeDtypeStruct((2, 2, row_cou...  20.3 us
    reshape x1, local copies, waits for them, and re-layouts, on_device(): state = contract_network(n, *parts, blocks).reshape(2, width, columns)  3.27 us

profile of v3, /device:TPU:1, one launch (start us, length us, event | category | flops | bytes accessed | tf_op | source)
XLA Modules:
  0.0 147.5 jit_solution(9370181237929447811)
XLA Ops:
  0.0 2.4 %copy.5 = bf16[16,32,2,512]{3,1,2,0:T(8,128)(2,1)} copy(bf16[16,32,2,512]{3,2,1,0:T(2,128)(2,1)} %bitcast.16) | data formatting | bytes 2097152 | tf_op jit(solution)/shard_map/reshape | solution.py:267
  2.4 10.2 %shard_map.47 = f32[2,2,512,512]{3,2,1,0:T(8,128)} custom-call(s32[4]{0:T(128)} %bits.3, bf16[4,2,512,2,512]{4,3,2,1,0:T(2,128)(2,1)} %left_ref.3, bf16[4,2,512,2,512]{4,3,2,1,0:T(2,128)(2,1)} %right_ref.3), custom_call_target="tpu_custom_call" | custom-call | tf_op jit(solution)/shard_map/pallas_call | solution.py:249
  12.6 10.1 %shard_map.46 = f32[2,2,512,512]{3,2,1,0:T(8,128)} custom-call(s32[4]{0:T(128)} %bits.3, bf16[4,2,512,2,512]{4,3,2,1,0:T(2,128)(2,1)} %left_ref.3, bf16[4,2,512,2,512]{4,3,2,1,0:T(2,128)(2,1)} %right_ref.3), custom_call_target="tpu_custom_call" | custom-call | tf_op jit(solution)/shard_map/pallas_call | solution.py:249
  22.7 121.5 %shard_map.48 = bf16[2,16,32,512]{3,2,1,0:T(8,128)(2,1)} custom-call(f32[4,16,32,512]{3,2,1,0:T(8,128)} %bitcast.13, f32[4,16,32,512]{3,2,1,0:T(8,128)} %bitcast.12, bf16[16,64,512]{2,1,0:T(8,128)(2,1)} %bitcast.15), custom_call_target="tpu_custom_call" | custom-call | tf_op jit(solution)/shard_map/pallas_call | solution.py:197
  144.3 3.3 %copy.8 = bf16[2,512,512]{2,0,1:T(2,128)(2,1)} copy(bf16[2,512,512]{2,1,0:T(8,128)(2,1)} %bitcast.14) | data formatting | bytes 2097152 | tf_op jit(solution)/shard_map/reshape | solution.py:271

commit v4 on v3

--- a/solution.py
+++ b/solution.py
@@ -8,22 +8,20 @@
 from jax.sharding import PartitionSpec as P
 
 ROUNDS = 2
-PLANES = 4
 TILES = 4
 LAG = 2
-EARLY = 4
-SPREAD = 0.8
-UNITS = 2
+EARLY = 12
+SPREAD = 0.4
+UNITS = 4
 MESH = pl.DeviceIdType.MESH
 
 
 def network_kernel(
-    n, part0, part1, blocks0, out, acc, outgoing, incoming, branch, got0, got1, blocks1, absorbed,
+    n, part, blocks0, out, acc, outgoing, incoming, branch, got0, got1, blocks1, absorbed,
     a_send, a_recv, r_send, r_recv,
 ):
-    planes = part0.shape[0]
-    chunks = 2 * planes
-    span, columns = part0.shape[2], part0.shape[3]
+    chunks, _, span, columns = part.shape
+    planes = chunks // ROUNDS
     width = n * span
     steps = n.bit_length() - 1
     tiles = TILES
@@ -72,11 +70,6 @@
 
         lax.fori_loop(1 if i == 0 else 0, group, one, 0)
 
-    def source(c, step):
-        if step:
-            return acc, c
-        return (part0, c) if c < planes else (part1, c - planes)
-
     def reduce_copy(c, s):
         half, at = n >> (s + 1), n - (n >> s)
         return pltpu.make_async_remote_copy(
@@ -93,8 +86,8 @@
     def begin(c, step):
         if step < steps:
             give = pl.ds(gives[step], n >> (step + 1))
-            ref, at = source(c, step)
-            outgoing[c, give] = ref[at, give].astype(outgoing.dtype)
+            source = acc if step else part
+            outgoing[c, give] = source[c, give].astype(outgoing.dtype)
             reduce_copy(c, step).start()
         else:
             s = 2 * steps - 1 - step
@@ -105,8 +98,8 @@
             half, at = n >> (step + 1), n - (n >> step)
             reduce_copy(c, step).wait_recv()
             keep = pl.ds(starts[step + 1], half)
-            ref, own = source(c, step)
-            total = ref[own, keep] + incoming[c, pl.ds(at, half)].astype(jnp.float32)
+            source = acc if step else part
+            total = source[c, keep] + incoming[c, pl.ds(at, half)].astype(jnp.float32)
             if step == steps - 1:
                 branch[c, keep] = total.astype(branch.dtype)
             else:
@@ -151,10 +144,11 @@
     order = [2, 1, 3, 0]
     sends = [(i, j) for i in order for j in range(group) if i or j]
     ready = planes - 1 + 2 * steps * LAG
-    entry = [c if c < planes else ready - EARLY + c - planes for c in range(chunks)]
+    turn = [(c + planes // 2) % planes for c in range(planes)]
+    entry = turn + [max(planes, ready - EARLY) + at for at in turn]
     work = [functools.partial(absorb, 0, i) for i in order] + [functools.partial(renew, i) for i in order]
     unsent = list(order)
-    total_slots = entry[-1] + 2 * steps * LAG + 1
+    total_slots = max(entry) + 2 * steps * LAG + 1
     for t in range(total_slots):
         for c in range(chunks):
             if t < entry[c] or (t - entry[c]) % LAG:
@@ -189,15 +183,15 @@
             gather_copy(c, s, starts[s + 1]).wait_send()
 
 
-def contract_network(n, part0, part1, blocks):
-    planes, _, span, columns = part0.shape
+def contract_network(n, part, blocks):
+    chunks, _, span, columns = part.shape
     steps = n.bit_length() - 1
-    both = (2 * planes,) + part0.shape[1:]
+    both = part.shape
     vmem = pl.BlockSpec(memory_space=pltpu.VMEM)
     return pl.pallas_call(
         functools.partial(network_kernel, n),
         out_shape=jax.ShapeDtypeStruct((2, n, span, columns), jnp.bfloat16),
-        in_specs=[vmem, vmem, vmem],
+        in_specs=[vmem, vmem],
         out_specs=vmem,
         scratch_shapes=[
             pltpu.VMEM(both, jnp.float32),
@@ -210,48 +204,50 @@
             pltpu.VMEM((2, n, span, columns), jnp.bfloat16),
             pltpu.SemaphoreType.DMA((2, n)),
             pltpu.SemaphoreType.DMA((2, n)),
-            pltpu.SemaphoreType.DMA((2 * planes, 2 * steps)),
-            pltpu.SemaphoreType.DMA((2 * planes, 2 * steps)),
+            pltpu.SemaphoreType.DMA((chunks, 2 * steps)),
+            pltpu.SemaphoreType.DMA((chunks, 2 * steps)),
         ],
         compiler_params=pltpu.CompilerParams(collective_id=0, has_side_effects=True),
-    )(part0, part1, blocks)
+    )(part, blocks)
+
+
+def leaf_product(plain_ref, other_ref, out_ref):
+    rows = 2 * plain_ref.shape[2]
+    plain = plain_ref[0, 0].reshape(rows, plain_ref.shape[4])
+    other = other_ref[0, 0].reshape(rows, other_ref.shape[4]).astype(jnp.float32)
+    even = lax.rem(lax.broadcasted_iota(jnp.int32, other.shape, 0), 2) == 0
+    signed = jnp.where(even, other, -other).astype(jnp.bfloat16)
+    swapped = jnp.where(even, pltpu.roll(other, rows - 1, 0), pltpu.roll(other, 1, 0)).astype(jnp.bfloat16)
+    dims = (((0,), (0,)), ((), ()))
+    out_ref[0, 0] = lax.dot_general(plain, signed, dims, preferred_element_type=jnp.float32)
+    out_ref[0, 1] = lax.dot_general(plain, swapped, dims, preferred_element_type=jnp.float32)
 
 
 def leaf_kernel(bits, left_ref, right_ref, out_ref):
-    depth, row_count = left_ref.shape[2], left_ref.shape[4]
-    width = right_ref.shape[4]
-    left = left_ref[0, 0].reshape(2 * depth, row_count)
-    right = right_ref[0, 0].reshape(2 * depth, width).astype(jnp.float32)
-    even = lax.rem(lax.broadcasted_iota(jnp.int32, right.shape, 0), 2) == 0
-    signed = jnp.where(even, right, -right).astype(jnp.bfloat16)
-    swapped = jnp.where(even, pltpu.roll(right, 2 * depth - 1, 0), pltpu.roll(right, 1, 0)).astype(jnp.bfloat16)
-    def product(a, b):
-        return lax.dot_general(a, b, (((0,), (0,)), ((), ())), preferred_element_type=jnp.float32)
-
-    @pl.when(pl.program_id(0) == 0)
+    transposed = lax.rem(pl.program_id(0), 2) == 0
+
+    @pl.when(transposed)
     def _():
-        out_ref[0, 0] = product(signed, left)
-        out_ref[0, 1] = product(swapped, left)
-
-    @pl.when(pl.program_id(0) != 0)
+        leaf_product(right_ref, left_ref, out_ref)
+
+    @pl.when(jnp.logical_not(transposed))
     def _():
-        out_ref[0, 0] = product(left, signed)
-        out_ref[0, 1] = product(left, swapped)
-
-
-def leaf_terms(bits, leaf_left, leaf_right, first):
-    _, _, depth, _, row_count = leaf_left.shape
+        leaf_product(left_ref, right_ref, out_ref)
+
+
+def leaf_terms(bits, leaf_left, leaf_right):
+    branches, _, depth, _, row_count = leaf_left.shape
     width = leaf_right.shape[4]
 
     def chosen(j, chosen_bits):
-        return (first + j, chosen_bits[first + j], 0, 0, 0)
+        return (j, chosen_bits[j], 0, 0, 0)
 
     return pl.pallas_call(
         leaf_kernel,
-        out_shape=jax.ShapeDtypeStruct((2, 2, row_count, width), jnp.float32),
+        out_shape=jax.ShapeDtypeStruct((branches, 2, row_count, width), jnp.float32),
         grid_spec=pltpu.PrefetchScalarGridSpec(
             num_scalar_prefetch=1,
-            grid=(2,),
+            grid=(branches,),
             in_specs=[
                 pl.BlockSpec((1, 1, depth, 2, row_count), chosen),
                 pl.BlockSpec((1, 1, depth, 2, width), chosen),
@@ -265,10 +261,8 @@
     width, columns = stem_tensor.shape[1], stem_tensor.shape[3]
     span = width // n
     blocks = jnp.transpose(stem_tensor.reshape(n, span, 2, columns), (0, 2, 1, 3)).reshape(n, 2 * span, columns)
-    parts = [
-        leaf_terms(slice_bits, leaf_left, leaf_right, 2 * r).reshape(PLANES, n, span, columns) for r in range(ROUNDS)
-    ]
-    state = contract_network(n, *parts, blocks).reshape(2, width, columns)
+    part = leaf_terms(slice_bits, leaf_left, leaf_right).reshape(-1, n, span, columns)
+    state = contract_network(n, part, blocks).reshape(2, width, columns)
     return jnp.transpose(state, (1, 0, 2))[None]
 
 

time: 148 us -> 115 us (0.78)
  Pallas kernels: 142 us -> 109 us
    pallas_call x1, Pallas kernels: 122 us -> 97.7 us  [contract_network(): pl.pallas_call(functools.partial(network_kernel, n), out_shape=jax.ShapeD...]
    pallas_call x2 -> x1, Pallas kernels: 20.3 us -> 11.6 us  [leaf_terms(): pl.pallas_call(leaf_kernel, out_shape=jax.ShapeDtypeStruct((branches, 2,...]
where the time goes in v4:
time: 115 us
  Pallas kernels  109 us (95%)
  local copies, waits for them, and re-layouts  5.69 us (5%)
    pallas_call x1, Pallas kernels, contract_network(): pl.pallas_call(functools.partial(network_kernel, n), out_shape=jax.ShapeD...  97.7 us
    pallas_call x1, Pallas kernels, leaf_terms(): pl.pallas_call(leaf_kernel, out_shape=jax.ShapeDtypeStruct((branches, 2,...  11.6 us
    reshape x1, local copies, waits for them, and re-layouts, on_device(): state = contract_network(n, part, blocks).reshape(2, width, columns)  3.27 us
    reshape x1, local copies, waits for them, and re-layouts, on_device(): stem_tensor.reshape(n, span, 2, columns)  2.42 us

profile of v4, /device:TPU:1, one launch (start us, length us, event | category | flops | bytes accessed | tf_op | source)
XLA Modules:
  0.0 115.1 jit_solution(11064567478601032673)
XLA Ops:
  0.0 2.4 %copy.5 = bf16[16,32,2,512]{3,1,2,0:T(8,128)(2,1)} copy(bf16[16,32,2,512]{3,2,1,0:T(2,128)(2,1)} %bitcast.14) | data formatting | bytes 2097152 | tf_op jit(solution)/shard_map/reshape | solution.py:263
  2.4 11.6 %shard_map.46 = f32[4,2,512,512]{3,2,1,0:T(8,128)} custom-call(s32[4]{0:T(128)} %bits.1, bf16[4,2,512,2,512]{4,3,2,1,0:T(2,128)(2,1)} %left_ref.1, bf16[4,2,512,2,512]{4,3,2,1,0:T(2,128)(2,1)} %right_ref.1), custom_call_target="tpu_custom_call" | custom-call | tf_op jit(solution)/shard_map/pallas_call | solution.py:245
  14.1 97.7 %shard_map.47 = bf16[2,16,32,512]{3,2,1,0:T(8,128)(2,1)} custom-call(f32[8,16,32,512]{3,2,1,0:T(8,128)} %bitcast.11, bf16[16,64,512]{2,1,0:T(8,128)(2,1)} %bitcast.13), custom_call_target="tpu_custom_call" | custom-call | tf_op jit(solution)/shard_map/pallas_call | solution.py:191
  111.8 3.3 %copy.8 = bf16[2,512,512]{2,0,1:T(2,128)(2,1)} copy(bf16[2,512,512]{2,1,0:T(8,128)(2,1)} %bitcast.12) | data formatting | bytes 2097152 | tf_op jit(solution)/shard_map/reshape | solution.py:265
